TPU v7x, 32 devices: a whole 2x2x4 slice. The times are simulated.
32 devices in a mesh: dp: 16 (over z, y, x), seq: 2 (over core).
Axes of the slice: x: 2, y: 2, z: 4, core: 2. Of those that a mesh axis runs over, the one named last changes fastest.
Arguments:
- latents: float32 [16, 256, 48], P('dp', 'seq'), may hold values from -6 to 6
- valid: int32 [16, 256], P('dp', 'seq'), may hold values 0 or 1
- class_labels: int32 [16], replicated, may hold values from 0 to 447
- group_perm: int32 [16], P('dp'), may hold values from 0 to 15, as said below
- patch_weight: bfloat16 [48, 768], replicated, may hold values from -0.875 to 0.875
- pos_table: bfloat16 [256, 768], P('seq'), may hold values from -3 to 3
- class_table: bfloat16 [1024, 768], replicated, may hold values from -3 to 3
- ln1_gain: bfloat16 [1, 768], replicated, may hold values from 0.25 to 1.75
- ln1_bias: bfloat16 [1, 768], replicated, may hold values from -1.5 to 1.5
- qkv_weight: bfloat16 [1, 768, 2304], replicated, may hold values from -0.21875 to 0.21875
- out_weight: bfloat16 [1, 768, 768], replicated, may hold values from -0.875 to 0.875
- ln2_gain: bfloat16 [1, 768], replicated, may hold values from 0.25 to 1.75
- ln2_bias: bfloat16 [1, 768], replicated, may hold values from -1.5 to 1.5
- up_weight: bfloat16 [1, 768, 3072], replicated, may hold values from -0.21875 to 0.21875
- up_bias: bfloat16 [1, 3072], replicated, may hold values from -1.5 to 1.5
- down_weight: bfloat16 [1, 3072, 768], replicated, may hold values from -0.109375 to 0.109375
- head_weight: bfloat16 [768, 96], replicated, may hold values from -0.109375 to 0.109375
- head_bias: bfloat16 [96], replicated, may hold values from -1 to 1
- cot_latents: float32 [16, 256, 48], P('dp', 'seq'), may hold values from -6 to 6
- cot_logdet: float32 [16], P('dp'), may hold values from -4 to 4
Outputs:
- new_latents: float32 [16, 256, 48], P('dp', 'seq')
- logdet: float32 [16], P('dp')
- latents_grad: float32 [16, 256, 48], P('dp', 'seq')
- patch_weight_grad: float32 [48, 768], replicated
- pos_grad: float32 [256, 768], P('seq')
- class_grad: float32 [1024, 768], P('dp')
- ln1_gain_grad: float32 [1, 768], replicated
- ln1_bias_grad: float32 [1, 768], replicated
- qkv_grad: float32 [1, 768, 2304], replicated
- out_grad: float32 [1, 768, 768], replicated
- ln2_gain_grad: float32 [1, 768], replicated
- ln2_bias_grad: float32 [1, 768], replicated
- up_grad: float32 [1, 768, 3072], replicated
- up_bias_grad: float32 [1, 3072], replicated
- down_grad: float32 [1, 3072, 768], replicated
- head_weight_grad: float32 [768, 96], replicated
- head_bias_grad: float32 [96], replicated
Inputs may be any that keep to these rules, and one draw needn't show every extreme that they name: Each of 0 to 15 once; class_labels[group_perm] never falls.
All inputs are finite; a program needn't handle non-finite values. No bound on the sum of `valid` on one device may be relied on, other than what follows from the above.
Results may differ from a plain program's by a relative error of at most 0.023.
Values may be sent and summed in bfloat16 or wider, within the bound.
A program may use at most 320 MiB of HBM per device.

v0:
```python
import jax
import jax.numpy as jnp
from jax import lax
from jax.sharding import PartitionSpec as P

HEAD_DIM = 64
precise = lax.Precision.HIGHEST
norm_eps = 1e-05


def shifted_2(shard, axis, by):
    size = lax.axis_size(axis)
    pairs = [(i, i + by) for i in range(size) if 0 <= i + by < size]
    return lax.ppermute(shard, axis, pairs)


def layer_norm(values, norm_gain, norm_bias):
    center = values - jnp.mean(values, -1, keepdims=True)
    spread = jnp.mean(center * center, -1, keepdims=True)
    return center * lax.rsqrt(spread + norm_eps) * norm_gain + norm_bias


def matmul(left_side, weight_mat):
    return jnp.dot(left_side, weight_mat, preferred_element_type=jnp.float32)


def outer_sum(left_side, grad_side):
    left_flat = left_side.reshape(-1, left_side.shape[-1])
    grad_flat = grad_side.reshape(-1, grad_side.shape[-1])
    return lax.dot_general(
        left_flat, grad_flat, (((0,), (0,)), ((), ())), preferred_element_type=jnp.float32
    )


def transposed(grad_side, weight_mat):
    return lax.dot_general(
        grad_side,
        weight_mat,
        (((grad_side.ndim - 1,), (1,)), ((), ())),
        preferred_element_type=jnp.float32,
    )


def eight_rows(matrix):
    return matrix.reshape(8, -1)


def attention_mask(key_valid, patch_rows, seq_place):
    query_pos = seq_place * patch_rows + lax.iota(jnp.int32, patch_rows)
    key_pos = (seq_place - 1) * patch_rows + lax.iota(jnp.int32, 2 * patch_rows)
    earlier = (key_pos[None, :] < query_pos[:, None])[None] & (key_valid[:, None, :] > 0)
    return earlier | (key_pos[None, :] == query_pos[:, None])[None]


def masked_scores(query, keys, allowed):
    logits = jnp.einsum(
        "bqhd,bkhd->bhqk", query, keys, preferred_element_type=jnp.float32
    ) * HEAD_DIM ** (-0.5)
    return jnp.where(allowed[:, None], logits, -1e30)


def forward(latents, valid, class_rows, seq_place, weights):
    (
        patch_weight,
        pos_table,
        qkv_weight,
        out_weight,
        ln1_gain,
        ln1_bias,
        ln2_gain,
        ln2_bias,
        up_weight,
        up_bias,
        down_weight,
        head_weight,
        head_bias,
    ) = weights
    images, patch_rows, channels = latents.shape
    model_width = qkv_weight.shape[1]
    head_count = model_width // HEAD_DIM
    latent_low = latents.astype(jnp.bfloat16)
    hidden = (
        matmul(latent_low, patch_weight)
        + pos_table.astype(jnp.float32)[None]
        + class_rows[:, None, :]
    )
    own_mask = valid.astype(jnp.bfloat16)
    normed = layer_norm(
        hidden, ln1_gain[0].astype(jnp.float32), ln1_bias[0].astype(jnp.float32)
    ).astype(jnp.bfloat16)
    packed = matmul(normed, qkv_weight[0]).astype(jnp.bfloat16)
    query = packed[..., :model_width].reshape(images, patch_rows, head_count, HEAD_DIM)
    keys_own = packed[..., model_width : 2 * model_width]
    values_own = packed[..., 2 * model_width :]
    prior_keys, prior_values, prior_mask = shifted_2((keys_own, values_own, own_mask), "seq", 1)
    keys = jnp.concatenate((prior_keys, keys_own), 1).reshape(
        images, 2 * patch_rows, head_count, HEAD_DIM
    )
    values = jnp.concatenate((prior_values, values_own), 1).reshape(
        images, 2 * patch_rows, head_count, HEAD_DIM
    )
    allowed = attention_mask(jnp.concatenate((prior_mask, own_mask), 1), patch_rows, seq_place)
    logits = masked_scores(query, keys, allowed)
    row_peak = jnp.max(logits, -1, keepdims=True)
    log_total = row_peak + jnp.log(jnp.sum(jnp.exp(logits - row_peak), -1, keepdims=True))
    weights_soft = jnp.exp(logits - log_total).astype(jnp.bfloat16)
    attended = jnp.einsum(
        "bhqk,bkhd->bqhd", weights_soft, values, preferred_element_type=jnp.float32
    )
    attended = attended.astype(jnp.bfloat16).reshape(images, patch_rows, model_width)
    mid = hidden + matmul(attended, out_weight[0])
    second = layer_norm(
        mid, ln2_gain[0].astype(jnp.float32), ln2_bias[0].astype(jnp.float32)
    ).astype(jnp.bfloat16)
    preact = matmul(second, up_weight[0]) + up_bias[0].astype(jnp.float32)
    activated = jax.nn.gelu(preact, approximate=True).astype(jnp.bfloat16)
    saved = [
        (
            hidden,
            normed,
            query,
            keys,
            values,
            allowed,
            log_total,
            attended,
            mid,
            second,
            preact,
            activated,
        )
    ]
    hidden = mid + matmul(activated, down_weight[0])
    top_low = hidden.astype(jnp.bfloat16)
    head_out = matmul(top_low, head_weight) + head_bias.astype(jnp.float32)
    prior_row = shifted_2(head_out[:, patch_rows - 1, :], "seq", 1)
    shifted = jnp.concatenate((prior_row[:, None, :], head_out[:, : patch_rows - 1, :]), 1)
    shifted = shifted * valid.astype(jnp.float32)[..., None]
    alpha = shifted[..., :channels]
    shift_mean = shifted[..., channels:]
    factor = jnp.exp(-alpha)
    new_latents = (latents - shift_mean) * factor
    logdet_part = -jnp.sum(alpha, (1, 2))
    return (new_latents, logdet_part, factor, top_low, saved)


def local(
    latents,
    valid,
    class_labels,
    group_perm,
    patch_weight,
    pos_table,
    class_table,
    ln1_gain,
    ln1_bias,
    qkv_weight,
    out_weight,
    ln2_gain,
    ln2_bias,
    up_weight,
    up_bias,
    down_weight,
    head_weight,
    head_bias,
    cot_latents,
    cot_logdet,
):
    images, patch_rows, channels = latents.shape
    model_width = qkv_weight.shape[1]
    head_count = model_width // HEAD_DIM
    layer_total = qkv_weight.shape[0]
    seq_place = lax.axis_index("seq")
    picks = group_perm[:, None] == lax.iota(jnp.int32, class_labels.shape[0])[None, :]
    image_labels = jnp.sum(jnp.where(picks, class_labels[None, :], 0), 1)
    label_hot = image_labels[:, None] == lax.iota(jnp.int32, class_table.shape[0])[None, :]
    class_rows = matmul(label_hot.astype(jnp.bfloat16), class_table)
    weights = (
        patch_weight,
        pos_table,
        qkv_weight,
        out_weight,
        ln1_gain,
        ln1_bias,
        ln2_gain,
        ln2_bias,
        up_weight,
        up_bias,
        down_weight,
        head_weight,
        head_bias,
    )
    new_latents, logdet_part, factor, top_low, saved = forward(
        latents, valid, class_rows, seq_place, weights
    )
    latents_again, unused = lax.optimization_barrier((latents, new_latents))
    unused_a, unused_b, unused_c, unused_d, saved = forward(
        latents_again, valid, class_rows, seq_place, weights
    )
    valid_float = valid.astype(jnp.float32)
    d_alpha = -cot_latents * new_latents - cot_logdet[:, None, None]
    d_mean = -cot_latents * factor
    d_shifted = jnp.concatenate((d_alpha, d_mean), -1) * valid_float[..., None]
    next_row = shifted_2(d_shifted[:, 0, :], "seq", -1)
    d_head = jnp.concatenate((d_shifted[:, 1:, :], next_row[:, None, :]), 1).astype(jnp.bfloat16)
    head_weight_grad = outer_sum(top_low, d_head)
    head_bias_grad = jnp.sum(d_head.astype(jnp.float32), (0, 1))
    d_hidden = transposed(d_head, head_weight)
    grads_qkv, grads_out, grads_up, grads_down = ([], [], [], [])
    grads_g1, grads_b1, grads_g2, grads_b2, grads_ub = ([], [], [], [], [])
    for layer_index in reversed(range(layer_total)):
        (
            hidden,
            normed,
            query,
            keys,
            values,
            allowed,
            log_total,
            attended,
            mid,
            second,
            preact,
            activated,
        ) = saved[layer_index]
        d_down = d_hidden.astype(jnp.bfloat16)
        down_grad = outer_sum(activated, d_down)
        d_act = transposed(d_down, down_weight[layer_index])
        unused_gelu, gelu_pull = jax.vjp(lambda inner: jax.nn.gelu(inner, approximate=True), preact)
        d_pre = gelu_pull(d_act)[0].astype(jnp.bfloat16)
        up_bias_grad = jnp.sum(d_pre.astype(jnp.float32), (0, 1))
        up_grad = outer_sum(second, d_pre)
        d_second = transposed(d_pre, up_weight[layer_index])
        unused_norm, norm_pull = jax.vjp(
            layer_norm,
            mid,
            ln2_gain[layer_index].astype(jnp.float32),
            ln2_bias[layer_index].astype(jnp.float32),
        )
        d_mid_norm, ln2_gain_part, ln2_bias_part = norm_pull(d_second)
        d_mid = d_hidden + d_mid_norm
        d_proj = d_mid.astype(jnp.bfloat16)
        out_grad = outer_sum(attended, d_proj)
        d_attended = transposed(d_proj, out_weight[layer_index]).astype(jnp.bfloat16)
        d_attended = d_attended.reshape(images, patch_rows, head_count, HEAD_DIM)
        logits = masked_scores(query, keys, allowed)
        probs = jnp.exp(logits - log_total)
        d_probs = jnp.einsum(
            "bqhd,bkhd->bhqk", d_attended, values, preferred_element_type=jnp.float32
        )
        d_scores = (probs * (d_probs - jnp.sum(d_probs * probs, -1, keepdims=True))).astype(
            jnp.bfloat16
        )
        d_query = jnp.einsum(
            "bhqk,bkhd->bqhd", d_scores, keys, preferred_element_type=jnp.float32
        ) * HEAD_DIM ** (-0.5)
        d_keys = jnp.einsum(
            "bhqk,bqhd->bkhd", d_scores, query, preferred_element_type=jnp.float32
        ) * HEAD_DIM ** (-0.5)
        d_values = jnp.einsum(
            "bhqk,bqhd->bkhd",
            probs.astype(jnp.bfloat16),
            d_attended,
            preferred_element_type=jnp.float32,
        )
        d_keys = d_keys.reshape(images, 2 * patch_rows, model_width)
        d_values = d_values.reshape(images, 2 * patch_rows, model_width)
        back_keys, back_values = (
            shifted_2(d_keys[:, :patch_rows].astype(jnp.bfloat16), "seq", -1).astype(jnp.float32),
            shifted_2(d_values[:, :patch_rows].astype(jnp.bfloat16), "seq", -1).astype(jnp.float32),
        )
        d_packed = jnp.concatenate(
            (
                d_query.reshape(images, patch_rows, model_width),
                d_keys[:, patch_rows:] + back_keys,
                d_values[:, patch_rows:] + back_values,
            ),
            -1,
        ).astype(jnp.bfloat16)
        qkv_grad = outer_sum(normed, d_packed)
        d_normed = transposed(d_packed, qkv_weight[layer_index])
        unused_norm, norm_pull = jax.vjp(
            layer_norm,
            hidden,
            ln1_gain[layer_index].astype(jnp.float32),
            ln1_bias[layer_index].astype(jnp.float32),
        )
        d_input, ln1_gain_part, ln1_bias_part = norm_pull(d_normed)
        d_hidden = d_mid + d_input
        grads_qkv.insert(0, qkv_grad)
        grads_out.insert(0, out_grad)
        grads_up.insert(0, up_grad)
        grads_down.insert(0, down_grad)
        grads_g1.insert(0, ln1_gain_part)
        grads_b1.insert(0, ln1_bias_part)
        grads_g2.insert(0, ln2_gain_part)
        grads_b2.insert(0, ln2_bias_part)
        grads_ub.insert(0, up_bias_grad)
    d_embed_low = d_hidden.astype(jnp.bfloat16)
    patch_grad_part = outer_sum(latents.astype(jnp.bfloat16), d_embed_low)
    latents_grad = cot_latents * factor + transposed(d_embed_low, patch_weight)
    pos_part = jnp.sum(d_hidden, 0)
    class_part = jnp.sum(d_hidden, 1)
    logdet, class_sums = lax.psum((logdet_part, class_part), "seq")
    class_term = lax.dot_general(
        label_hot.astype(jnp.float32),
        class_sums,
        (((0,), (0,)), ((), ())),
        precision=precise,
        preferred_element_type=jnp.float32,
    )
    class_grad = lax.psum_scatter(class_term, "dp", scatter_dimension=0, tiled=True)
    pos_grad = lax.psum(pos_part, "dp")
    (
        patch_weight_grad,
        head_weight_grad,
        head_bias_grad,
        ln1_gain_grad,
        ln1_bias_grad,
        ln2_gain_grad,
        ln2_bias_grad,
        up_bias_grad,
    ) = lax.psum(
        (
            patch_grad_part,
            head_weight_grad,
            head_bias_grad,
            jnp.stack(grads_g1),
            jnp.stack(grads_b1),
            jnp.stack(grads_g2),
            jnp.stack(grads_b2),
            jnp.stack(grads_ub),
        ),
        ("dp", "seq"),
    )
    qkv_stack = jnp.stack(grads_qkv)
    out_stack = jnp.stack(grads_out)
    up_stack = jnp.stack(grads_up)
    down_stack = jnp.stack(grads_down)
    flat_parts = (
        lax.psum_scatter(eight_rows(qkv_stack), ("dp", "seq"), scatter_dimension=1, tiled=True),
        lax.psum_scatter(eight_rows(out_stack), ("dp", "seq"), scatter_dimension=1, tiled=True),
        lax.psum_scatter(eight_rows(up_stack), ("dp", "seq"), scatter_dimension=1, tiled=True),
        lax.psum_scatter(eight_rows(down_stack), ("dp", "seq"), scatter_dimension=1, tiled=True),
    )
    flat_qkv, flat_out, flat_up, flat_down = (
        lax.all_gather(
            flat_parts[0].astype(jnp.bfloat16), ("dp", "seq"), axis=1, tiled=True
        ).astype(jnp.float32),
        lax.all_gather(
            flat_parts[1].astype(jnp.bfloat16), ("dp", "seq"), axis=1, tiled=True
        ).astype(jnp.float32),
        lax.all_gather(
            flat_parts[2].astype(jnp.bfloat16), ("dp", "seq"), axis=1, tiled=True
        ).astype(jnp.float32),
        lax.all_gather(
            flat_parts[3].astype(jnp.bfloat16), ("dp", "seq"), axis=1, tiled=True
        ).astype(jnp.float32),
    )
    qkv_stack = flat_qkv.reshape(qkv_stack.shape)
    out_stack = flat_out.reshape(out_stack.shape)
    up_stack = flat_up.reshape(up_stack.shape)
    down_stack = flat_down.reshape(down_stack.shape)
    return (
        new_latents,
        logdet,
        latents_grad,
        patch_weight_grad,
        pos_grad,
        class_grad,
        ln1_gain_grad,
        ln1_bias_grad,
        qkv_stack,
        out_stack,
        ln2_gain_grad,
        ln2_bias_grad,
        up_stack,
        up_bias_grad,
        down_stack,
        head_weight_grad,
        head_bias_grad,
    )


def solution(mesh):
    in_specs = (
        P("dp", "seq", None),
        P("dp", "seq"),
        P(),
        P("dp"),
        P(),
        P("seq", None),
        P(),
        P(),
        P(),
        P(),
        P(),
        P(),
        P(),
        P(),
        P(),
        P(),
        P(),
        P(),
        P("dp", "seq", None),
        P("dp"),
    )
    out_specs = (
        P("dp", "seq", None),
        P("dp"),
        P("dp", "seq", None),
        P(),
        P("seq", None),
        P("dp", None),
        P(),
        P(),
        P(),
        P(),
        P(),
        P(),
        P(),
        P(),
        P(),
        P(),
        P(),
    )
    return jax.shard_map(local, mesh=mesh, in_specs=in_specs, out_specs=out_specs, check_vma=False)
```

profile of v0, /device:TPU:0, one launch (start us, length us, event | category | flops | bytes accessed | tf_op | source)
XLA Modules:
  0.0 1260.5 jit_solution(11902922079995836065)
XLA Ops:
  14.1 3.0 collective-permute-start.2
  17.6 1.9 collective-permute-start.1
  19.5 2.0 collective-permute-start
  31.4 1.9 copy.53
  38.9 1.9 copy.51
  40.9 2.1 convolution_convert_fusion.3
  44.9 6.5 fusion.57
  57.1 2.0 multiply_subtract_fusion
  64.6 2.9 collective-permute-start.6
  70.5 4.3 collective-permute-start.5
  74.8 2.0 fusion.109
  78.6 1.9 copy.58
  85.6 1.9 copy.56
  87.5 2.1 convolution_convert_fusion.2
  90.4 3.3 fusion.13
  93.8 5.5 convert_reduce_fusion
  99.3 2.3 multiply_reduce_fusion.1
  102.7 1.9 fusion.96
  104.6 3.5 reshape_stack.13
  108.2 2.6 fusion.60
  112.5 2.5 multiply_reduce_fusion
  122.5 4.2 fusion.76
  126.7 7.2 reshape_stack.12
  134.6 6.5 fusion.125
  141.1 9.2 reshape_stack.14
  150.4 6.8 fusion.66
  157.2 9.3 reshape_stack.15
  166.6 42.8 %reduce-scatter.10.cloned.1.call-done = f32[8,2304]{1,0:T(8,128)} async-done(((f32[8,73728]{1,0:T(8,128)}), f32[8,2304]{1,0:T(8,128)}) %reduce-scatter.10.cloned.1.call-update) | async-done | bytes 73744 | tf_op jit(solution)/shard_map/reduce_scatter | solution.py:342
  211.0 123.2 %reduce-scatter.8.cloned.1.call-done = f32[8,6912]{1,0:T(8,128)} async-done(((f32[8,221184]{1,0:T(8,128)}), f32[8,6912]{1,0:T(8,128)}) %reduce-scatter.8.cloned.1.call-update) | async-done | bytes 221200 | tf_op jit(solution)/shard_map/reduce_scatter | solution.py:341
  335.8 139.6 %reduce-scatter.12.cloned.1.call-done = f32[8,9216]{1,0:T(8,128)} async-done(((f32[8,294912]{1,0:T(8,128)}), f32[8,9216]{1,0:T(8,128)}) %reduce-scatter.12.cloned.1.call-update) | async-done | bytes 294928 | tf_op jit(solution)/shard_map/reduce_scatter | solution.py:343
  477.1 139.7 %reduce-scatter.14.cloned.1.call-done = f32[8,9216]{1,0:T(8,128)} async-done(((f32[8,294912]{1,0:T(8,128)}), f32[8,9216]{1,0:T(8,128)}) %reduce-scatter.14.cloned.1.call-update) | async-done | bytes 294928 | tf_op jit(solution)/shard_map/reduce_scatter | solution.py:344
  618.5 1.9 fusion.108
  620.5 3.4 multiply_reduce_fusion.2
  624.9 1.8 convolution_bitcast_fusion
  626.8 1.9 fusion.65
  630.6 3.6 all-reduce.2
  634.2 1.9 broadcast_multiply_fusion
  639.2 41.3 %all-reduce = (f32[1,768]{1,0:T(1,128)}, f32[1,768]{1,0:T(1,128)}, f32[1,768]{1,0:T(1,128)}, f32[1,768]{1,0:T(1,128)}, f32[1,3072]{1,0:T(1,128)}, /*index=5*/f32[96]{0:T(128)}) all-reduce(f32[1,768]{1,0:T(1,128)S(1)} %stack.15, f32[1,768]{1,0:T(1,128)S(1)} %stack.16, ...), channel_id=1, replica_groups=mesh['dp'=16,'seq'=2] {'dp','seq'}, use_global_device_ids=true, to_apply=%region_26.27 | all-reduce | flops 6240 | bytes 49920 | tf_op jit(solution)/shard_map/psum | solution.py:323
  680.5 3.1 reshape.960
  683.6 51.8 %all-gather.5.cloned.1.call-done = bf16[8,221184]{1,0:T(8,128)(2,1)} async-done(((bf16[8,6912]{1,0:T(8,128)(2,1)}), bf16[8,221184]{1,0:T(8,128)(2,1)}) %all-gather.5.cloned.1.call-update) | async-done | bytes 3538960 | tf_op jit(solution)/shard_map/all_gather | solution.py:347
  735.4 6.3 reshape.958
  741.8 59.6 %all-gather.9.cloned.1.call-done = bf16[8,294912]{1,0:T(8,128)(2,1)} async-done(((bf16[8,9216]{1,0:T(8,128)(2,1)}), bf16[8,294912]{1,0:T(8,128)(2,1)}) %all-gather.9.cloned.1.call-update) | async-done | bytes 4718608 | tf_op jit(solution)/shard_map/all_gather | solution.py:353
  801.4 7.9 reshape.962
  809.3 57.4 %all-gather.11.cloned.1.call-done = bf16[8,294912]{1,0:T(8,128)(2,1)} async-done(((bf16[8,9216]{1,0:T(8,128)(2,1)}), bf16[8,294912]{1,0:T(8,128)(2,1)}) %all-gather.11.cloned.1.call-update) | async-done | bytes 4718608 | tf_op jit(solution)/shard_map/all_gather | solution.py:356
  866.7 7.9 reshape.964
  874.6 123.7 %all-reduce.8.cloned.1.call-done = (f32[48,768]{1,0:T(8,128)}, f32[768,96]{0,1:T(8,128)}) async-done(((f32[48,768]{1,0:T(8,128)}, f32[768,96]{0,1:T(8,128)}), (f32[48,768]{1,0:T(8,128)}, f32[768,96]{0,1:T(8,128)})) %all-reduce.8.cloned.1.call-update) | async-done | bytes 442384 | tf_op jit(solution)/shard_map/psum | solution.py:323
  998.3 115.3 %all-reduce.6.cloned.1.call-done = f32[128,768]{1,0:T(8,128)} async-done(((f32[128,768]{1,0:T(8,128)}), f32[128,768]{1,0:T(8,128)}) %all-reduce.6.cloned.1.call-update) | async-done | bytes 393232 | tf_op jit(solution)/shard_map/psum | solution.py:313
  1113.7 135.2 %reduce-scatter.6.cloned.1.call-done = f32[64,768]{1,0:T(8,128)} async-done(((f32[1024,768]{1,0:T(8,128)}), f32[64,768]{1,0:T(8,128)}) %reduce-scatter.6.cloned.1.call-update) | async-done | bytes 196624 | tf_op jit(solution)/shard_map/reduce_scatter | solution.py:312
  (236 shorter events, 72.8 us)
Async XLA Ops:
  7.2 5.4 copy-start
  7.2 5.3 copy-start.51
  7.2 5.3 copy-start.50
  7.2 202.2 %reduce-scatter.10.cloned.1.call-start = ((), (), s32[]{:S(2)}) async-start(), calls=%async_computation.9 | async-start | bytes 2433024 | tf_op jit(solution)/shard_map/reduce_scatter | solution.py:342
  7.3 4.6 copy-start.23
  7.3 4.6 copy-start.27
  7.3 4.6 copy-start.29
  12.5 50.5 %copy-start.32 = (f32[768]{0:T(1024)}, f32[768]{0:T(1024)S(1)}, u32[]{:S(2)}) copy-start(f32[768]{0:T(1024)S(1)} %get-tuple-element.71) | copy-start | bytes 9220
  12.6 4.6 copy-start.55
  14.1 15.5 %collective-permute-start.2 = (bf16[1,128,768]{2,1,0:T(8,128)(2,1)}, bf16[1,128,768]{2,1,0:T(8,128)(2,1)}, u32[]{:S(2)}, u32[]{:S(2)}) collective-permute-start(bf16[1,128,768]{2,1,0:T(8,128)(2,1)} %get-tuple-element.46), channel_id=1, source_target_pairs={{0,1},{2,3},{4,5},{6,7},{8,9},{10,11},{12,13},{14,15},{16,17},{18,... | collective-permute-start | bytes 589832 | tf_op jit(solution)/shard_map/ppermute | solution.py:14
  17.6 9.9 collective-permute-start.1
  19.5 17.6 %collective-permute-start = (bf16[1,128,768]{2,1,0:T(8,128)(2,1)}, bf16[1,128,768]{2,1,0:T(8,128)(2,1)}, u32[]{:S(2)}, u32[]{:S(2)}) collective-permute-start(bf16[1,128,768]{2,1,0:T(8,128)(2,1)} %get-tuple-element.48), channel_id=1, source_target_pairs={{0,1},{2,3},{4,5},{6,7},{8,9},{10,11},{12,13},{14,15},{16,17},{18,... | collective-permute-start | bytes 589832 | tf_op jit(solution)/shard_map/ppermute | solution.py:14
  23.3 21.6 %copy-start.34 = (f32[768]{0:T(1024)}, f32[768]{0:T(1024)S(1)}, u32[]{:S(2)}) copy-start(f32[768]{0:T(1024)S(1)} %get-tuple-element.73) | copy-start | bytes 9220
  53.3 2.1 collective-permute-start.3
  59.7 2.8 copy-start.30
  64.6 12.2 collective-permute-start.6
  67.5 7.3 collective-permute-start.4
  70.5 13.3 %collective-permute-start.5 = (bf16[1,128,768]{2,1,0:T(8,128)(2,1)}, bf16[1,128,768]{2,1,0:T(8,128)(2,1)}, u32[]{:S(2)}, u32[]{:S(2)}) collective-permute-start(bf16[1,128,768]{2,1,0:T(8,128)(2,1)} %get-tuple-element.45), channel_id=1, source_target_pairs={{0,1},{2,3},{4,5},{6,7},{8,9},{10,11},{12,13},{14,15},{16,17},{18,... | collective-permute-start | bytes 589832 | tf_op jit(solution)/shard_map/ppermute | solution.py:14
  80.6 3.3 copy-start.22
  90.1 11.5 copy-start.7
  90.1 11.5 copy-start.39
  90.4 11.3 copy-start.46
  90.4 3.4 copy-start.17
  90.4 8.9 slice-start
  93.8 5.5 copy-start.11
  93.8 5.5 slice-start.1
  108.1 226.0 %reduce-scatter.8.cloned.1.call-start = ((), (), s32[]{:S(2)}) async-start(), calls=%async_computation.7 | async-start | bytes 7299072 | tf_op jit(solution)/shard_map/reduce_scatter | solution.py:341
  116.3 3.4 copy-start.16
  116.3 3.9 collective-permute-start.7
  118.3 4.3 copy-start.5
  118.3 4.3 copy-start.33
  118.3 4.2 copy-start.44
  118.3 4.2 copy-start.48
  118.3 3.5 collective-permute-start.8
  133.9 341.5 %reduce-scatter.12.cloned.1.call-start = ((), (), s32[]{:S(2)}) async-start(), calls=%async_computation.11 | async-start | bytes 9732096 | tf_op jit(solution)/shard_map/reduce_scatter | solution.py:343
  150.4 466.4 %reduce-scatter.14.cloned.1.call-start = ((), (), s32[]{:S(2)}) async-start(), calls=%async_computation.13 | async-start | bytes 9732096 | tf_op jit(solution)/shard_map/reduce_scatter | solution.py:344
  166.5 453.9 %copy-start.45 = (f32[128]{0:T(128)S(1)}, f32[128]{0:T(128)}, u32[]{:S(2)}) copy-start(f32[128]{0:T(128)} %copy-done.43) | copy-start | bytes 1540
  166.5 453.9 %copy-start.49 = (f32[128]{0:T(128)S(1)}, f32[128]{0:T(128)}, u32[]{:S(2)}) copy-start(f32[128]{0:T(128)} %copy-done.47) | copy-start | bytes 1540
  166.6 513.9 %all-gather.7.cloned.1.call-start = ((), (), s32[]{:S(2)}) async-start(), calls=%async_computation.10 | async-start | bytes 1216512 | tf_op jit(solution)/shard_map/all_gather | solution.py:350
  210.9 524.5 %all-gather.5.cloned.1.call-start = ((), (), s32[]{:S(2)}) async-start(), calls=%async_computation.8 | async-start | bytes 3649536 | tf_op jit(solution)/shard_map/all_gather | solution.py:347
  335.8 465.6 %all-gather.9.cloned.1.call-start = ((), (), s32[]{:S(2)}) async-start(), calls=%async_computation.12 | async-start | bytes 4866048 | tf_op jit(solution)/shard_map/all_gather | solution.py:353
  477.1 389.6 %all-gather.11.cloned.1.call-start = ((), (), s32[]{:S(2)}) async-start(), calls=%async_computation.14 | async-start | bytes 4866048 | tf_op jit(solution)/shard_map/all_gather | solution.py:356
  618.5 379.9 %all-reduce.8.cloned.1.call-start = ((), (), s32[]{:S(2)}) async-start(), calls=%async_computation.15 | async-start | bytes 884736 | tf_op jit(solution)/shard_map/psum | solution.py:323
  620.4 3.4 copy-start.53
  620.4 3.4 copy-start.6
  620.4 3.6 copy-start.15
  628.7 485.0 %all-reduce.6.cloned.1.call-start = ((), (), s32[]{:S(2)}) async-start(), calls=%async_computation.5 | async-start | bytes 786432 | tf_op jit(solution)/shard_map/psum | solution.py:313
  629.2 619.7 %reduce-scatter.6.cloned.1.call-start = ((), (), s32[]{:S(2)}) async-start(), calls=%async_computation.6 | async-start | bytes 3342336 | tf_op jit(solution)/shard_map/reduce_scatter | solution.py:312
  (30 other events, 40.5 us)
Sparse Core Ops, SparseCore 0:
  108.3 101.0 reduce-scatter.9
  216.0 118.1 reduce-scatter.7
  340.6 134.7 reduce-scatter.11
  482.2 134.5 reduce-scatter.13
  619.6 53.5 all-gather.6
  676.5 58.9 all-gather.4
  738.9 62.4 all-gather.8
  804.3 62.4 all-gather.10
  873.2 125.0 all-reduce.7
  1004.8 108.8 all-reduce.5
  1119.2 129.6 reduce-scatter.5
where the time goes:
time: 1260 us
  waiting for transfers between devices  991 us (79%)
  local copies, waits for them, and re-layouts  84.4 us (7%)
  matrix products  68.3 us (5%)
  blocking collectives  44.9 us (4%)
  other arithmetic  34.9 us (3%)
  starting transfers between devices  20.1 us (2%)
  between operations  17 us (1%)
    reduce_scatter x1, waiting for transfers between devices, local(): lax.psum_scatter(eight_rows(down_stack), ('dp', 'seq'), scatter_dimension...  140 us
    reduce_scatter x1, waiting for transfers between devices, local(): lax.psum_scatter(eight_rows(up_stack), ('dp', 'seq'), scatter_dimension=1...  140 us
    reduce_scatter x1, waiting for transfers between devices, local(): lax.psum_scatter(class_term, 'dp', scatter_dimension=0, tiled=True)  135 us
    psum x1, waiting for transfers between devices, local(): lax.psum((patch_grad_part, head_weight_grad, head_bias_grad, jnp.stack(gr...  124 us
    reduce_scatter x1, waiting for transfers between devices, local(): lax.psum_scatter(eight_rows(qkv_stack), ('dp', 'seq'), scatter_dimension=...  123 us
    psum x1, waiting for transfers between devices, local(): pos_grad = lax.psum(pos_part, 'dp')  115 us
    all_gather x1, waiting for transfers between devices, local(): lax.all_gather(flat_parts[2].astype(jnp.bfloat16), ('dp', 'seq'), axis=1,...  59.6 us
    all_gather x1, waiting for transfers between devices, local(): lax.all_gather(flat_parts[3].astype(jnp.bfloat16), ('dp', 'seq'), axis=1,...  57.4 us
  transfers between devices with their start and end apart: 20, of which 12 were waited for; matrix products, arithmetic and copies ran while one was open for 10% of the time, Pallas kernels for 0%

commit v1 on v0

--- a/solution.py
+++ b/solution.py
@@ -321,17 +321,20 @@
         ln2_bias_grad,
         up_bias_grad,
     ) = lax.psum(
-        (
-            patch_grad_part,
-            head_weight_grad,
-            head_bias_grad,
-            jnp.stack(grads_g1),
-            jnp.stack(grads_b1),
-            jnp.stack(grads_g2),
-            jnp.stack(grads_b2),
-            jnp.stack(grads_ub),
+        lax.psum(
+            (
+                patch_grad_part,
+                head_weight_grad,
+                head_bias_grad,
+                jnp.stack(grads_g1),
+                jnp.stack(grads_b1),
+                jnp.stack(grads_g2),
+                jnp.stack(grads_b2),
+                jnp.stack(grads_ub),
+            ),
+            "seq",
         ),
-        ("dp", "seq"),
+        "dp",
     )
     qkv_stack = jnp.stack(grads_qkv)
     out_stack = jnp.stack(grads_out)

time: 1260 us -> 916 us (0.73)
  waiting for transfers between devices: 991 us -> 604 us
  blocking collectives: 44.9 us -> 80.6 us
    psum x1, waiting for transfers between devices: 124 us -> 0.01 us  [local(): lax.psum((patch_grad_part, head_weight_grad, head_bias_grad, jnp.stack(gr...]
    reduce_scatter x1, waiting for transfers between devices: 135 us -> 15.5 us  [local(): lax.psum_scatter(class_term, 'dp', scatter_dimension=0, tiled=True)]
    psum x1, waiting for transfers between devices: 115 us -> 0.01 us  [local(): lax.psum(lax.psum((patch_grad_part, head_weight_grad, head_bias_grad, jnp...]
    psum x1, blocking collectives: 41.3 us -> 75.4 us  [local(): lax.psum(lax.psum((patch_grad_part, head_weight_grad, head_bias_grad, jnp...]
    all_gather x1, waiting for transfers between devices: 51.8 us -> 25.6 us  [local(): lax.all_gather(flat_parts[0].astype(jnp.bfloat16), ('dp', 'seq'), axis=1,...]
  transfers between devices with their start and end apart: 20 -> 20, of which waited for: 12 -> 10; matrix products, arithmetic and copies ran while one was open for 10% -> 14% of each run, Pallas kernels for 0% -> 0%
where the time goes in v1:
time: 916 us; the launch traced here: 914 us
  waiting for transfers between devices  604 us (66%)
  local copies, waits for them, and re-layouts  88.4 us (10%)
  blocking collectives  80.6 us (9%)
  matrix products  67.3 us (7%)
  other arithmetic  34.9 us (4%)
  starting transfers between devices  20 us (2%)
  between operations  18.9 us (2%)
    reduce_scatter x1, waiting for transfers between devices, local(): lax.psum_scatter(eight_rows(up_stack), ('dp', 'seq'), scatter_dimension=1...  140 us
    reduce_scatter x1, waiting for transfers between devices, local(): lax.psum_scatter(eight_rows(down_stack), ('dp', 'seq'), scatter_dimension...  139 us
    reduce_scatter x1, waiting for transfers between devices, local(): lax.psum_scatter(eight_rows(qkv_stack), ('dp', 'seq'), scatter_dimension=...  123 us
    psum x1, blocking collectives, local(): lax.psum(lax.psum((patch_grad_part, head_weight_grad, head_bias_grad, jnp...  75.4 us
    all_gather x1, waiting for transfers between devices, local(): lax.all_gather(flat_parts[2].astype(jnp.bfloat16), ('dp', 'seq'), axis=1,...  62.3 us
    all_gather x1, waiting for transfers between devices, local(): lax.all_gather(flat_parts[3].astype(jnp.bfloat16), ('dp', 'seq'), axis=1,...  59.9 us
    reduce_scatter x1, waiting for transfers between devices, local(): lax.psum_scatter(eight_rows(out_stack), ('dp', 'seq'), scatter_dimension=...  35.4 us
    another operation x4, local copies, waits for them, and re-layouts, eight_rows(): return matrix.reshape(8, -1)  29.2 us
  transfers between devices with their start and end apart: 20, of which 10 were waited for; matrix products, arithmetic and copies ran while one was open for 14% of the time, Pallas kernels for 0%

profile of v1, /device:TPU:0, one launch (start us, length us, event | category | flops | bytes accessed | tf_op | source)
XLA Modules:
  0.0 913.6 jit_solution(12029548943059434236)
XLA Ops:
  14.9 3.0 collective-permute-start.2
  18.5 1.8 collective-permute-start.1
  20.3 2.0 collective-permute-start
  30.4 1.8 pad_maximum_fusion.2
  32.2 1.9 copy.53
  37.9 1.8 pad_maximum_fusion.1
  39.7 1.9 copy.51
  41.6 2.1 convolution_convert_fusion.3
  45.6 6.5 fusion.57
  57.8 2.0 multiply_subtract_fusion
  65.4 2.9 collective-permute-start.6
  71.3 4.3 collective-permute-start.5
  75.6 2.0 fusion.109
  77.6 1.8 pad_maximum_fusion.4
  79.4 1.9 copy.58
  86.3 1.9 copy.56
  88.2 2.1 convolution_convert_fusion.2
  91.1 3.3 fusion.13
  94.5 5.5 convert_reduce_fusion
  100.0 2.3 multiply_reduce_fusion.1
  103.5 1.9 fusion.96
  105.4 3.5 reshape_stack.13
  108.9 2.6 fusion.60
  113.3 2.5 multiply_reduce_fusion
  123.3 4.2 fusion.76
  127.5 7.2 reshape_stack.12
  135.4 6.5 fusion.125
  141.9 9.2 %reshape_stack.14 = f32[8,294912]{1,0:T(8,128)} reshape(f32[768,3072]{1,0:T(8,128)} %fusion.125) | data formatting | bytes 18874368 | tf_op jit(solution)/shard_map/reshape;stack | solution.py:45
  151.2 6.8 fusion.66
  158.0 9.3 %reshape_stack.15 = f32[8,294912]{1,0:T(8,128)} reshape(f32[3072,768]{1,0:T(8,128)} %fusion.66) | data formatting | bytes 18874368 | tf_op jit(solution)/shard_map/reshape;stack | solution.py:45
  167.3 1.9 fusion.108
  169.3 3.4 multiply_reduce_fusion.2
  174.7 35.4 %reduce-scatter.10.cloned.1.call-done = f32[8,2304]{1,0:T(8,128)} async-done(((f32[8,73728]{1,0:T(8,128)}), f32[8,2304]{1,0:T(8,128)}) %reduce-scatter.10.cloned.1.call-update) | async-done | bytes 73744 | tf_op jit(solution)/shard_map/reduce_scatter | solution.py:345
  211.7 123.2 %reduce-scatter.8.cloned.1.call-done = f32[8,6912]{1,0:T(8,128)} async-done(((f32[8,221184]{1,0:T(8,128)}), f32[8,6912]{1,0:T(8,128)}) %reduce-scatter.8.cloned.1.call-update) | async-done | bytes 221200 | tf_op jit(solution)/shard_map/reduce_scatter | solution.py:344
  336.6 139.7 %reduce-scatter.12.cloned.1.call-done = f32[8,9216]{1,0:T(8,128)} async-done(((f32[8,294912]{1,0:T(8,128)}), f32[8,9216]{1,0:T(8,128)}) %reduce-scatter.12.cloned.1.call-update) | async-done | bytes 294928 | tf_op jit(solution)/shard_map/reduce_scatter | solution.py:346
  478.1 139.5 %reduce-scatter.14.cloned.1.call-done = f32[8,9216]{1,0:T(8,128)} async-done(((f32[8,294912]{1,0:T(8,128)}), f32[8,9216]{1,0:T(8,128)}) %reduce-scatter.14.cloned.1.call-update) | async-done | bytes 294928 | tf_op jit(solution)/shard_map/reduce_scatter | solution.py:347
  619.2 1.9 fusion.65
  628.4 5.2 all-reduce.2
  633.6 2.6 broadcast_multiply_fusion
  636.9 75.4 %all-reduce = (f32[1,768]{1,0:T(1,128)}, f32[1,768]{1,0:T(1,128)}, f32[1,768]{1,0:T(1,128)}, f32[1,768]{1,0:T(1,128)}, f32[1,3072]{1,0:T(1,128)}, /*index=5*/f32[96]{0:T(128)}) all-reduce(f32[1,768]{1,0:T(1,128)S(1)} %copy-done.55, f32[1,768]{1,0:T(1,128)} %get-tuple-element.37, ...), channel_id=1, replica_groups=mesh['dp'=16,'seq'=2] {'dp'}, use_global_device_ids=true, to_apply=%region_28.29 | all-reduce | flops 6240 | bytes 49920 | tf_op jit(solution)/shard_map/psum | solution.py:323
  712.3 3.1 reshape.960
  715.4 25.6 %all-gather.5.cloned.1.call-done = bf16[8,221184]{1,0:T(8,128)(2,1)} async-done(((bf16[8,6912]{1,0:T(8,128)(2,1)}), bf16[8,221184]{1,0:T(8,128)(2,1)}) %all-gather.5.cloned.1.call-update) | async-done | bytes 3538960 | tf_op jit(solution)/shard_map/all_gather | solution.py:350
  741.1 6.3 reshape.958
  747.4 62.3 %all-gather.9.cloned.1.call-done = bf16[8,294912]{1,0:T(8,128)(2,1)} async-done(((bf16[8,9216]{1,0:T(8,128)(2,1)}), bf16[8,294912]{1,0:T(8,128)(2,1)}) %all-gather.9.cloned.1.call-update) | async-done | bytes 4718608 | tf_op jit(solution)/shard_map/all_gather | solution.py:356
  809.6 7.9 reshape.962
  817.6 59.9 %all-gather.11.cloned.1.call-done = bf16[8,294912]{1,0:T(8,128)(2,1)} async-done(((bf16[8,9216]{1,0:T(8,128)(2,1)}), bf16[8,294912]{1,0:T(8,128)(2,1)}) %all-gather.11.cloned.1.call-update) | async-done | bytes 4718608 | tf_op jit(solution)/shard_map/all_gather | solution.py:359
  877.5 8.0 reshape.964
  885.5 15.5 %reduce-scatter.6.cloned.1.call-done = f32[64,768]{1,0:T(8,128)} async-done(((f32[1024,768]{1,0:T(8,128)}), f32[64,768]{1,0:T(8,128)}) %reduce-scatter.6.cloned.1.call-update) | async-done | bytes 196624 | tf_op jit(solution)/shard_map/reduce_scatter | solution.py:312
  (244 shorter events, 71.4 us)
Async XLA Ops:
  8.0 5.4 copy-start
  8.0 5.3 copy-start.54
  8.0 5.3 copy-start.53
  8.1 202.1 %reduce-scatter.10.cloned.1.call-start = ((), (), s32[]{:S(2)}) async-start(), calls=%async_computation.8 | async-start | bytes 2433024 | tf_op jit(solution)/shard_map/reduce_scatter | solution.py:345
  8.1 4.6 copy-start.24
  8.1 4.6 copy-start.28
  8.1 4.6 copy-start.30
  13.4 50.5 %copy-start.34 = (f32[768]{0:T(1024)}, f32[768]{0:T(1024)S(1)}, u32[]{:S(2)}) copy-start(f32[768]{0:T(1024)S(1)} %get-tuple-element.80) | copy-start | bytes 9220
  13.4 4.6 copy-start.59
  14.9 15.4 %collective-permute-start.2 = (bf16[1,128,768]{2,1,0:T(8,128)(2,1)}, bf16[1,128,768]{2,1,0:T(8,128)(2,1)}, u32[]{:S(2)}, u32[]{:S(2)}) collective-permute-start(bf16[1,128,768]{2,1,0:T(8,128)(2,1)} %get-tuple-element.55), channel_id=1, source_target_pairs={{0,1},{2,3},{4,5},{6,7},{8,9},{10,11},{12,13},{14,15},{16,17},{18,... | collective-permute-start | bytes 589832 | tf_op jit(solution)/shard_map/ppermute | solution.py:14
  18.5 9.8 %collective-permute-start.1 = (bf16[1,128]{1,0:T(2,128)(2,1)}, bf16[1,128]{1,0:T(2,128)(2,1)}, u32[]{:S(2)}, u32[]{:S(2)}) collective-permute-start(bf16[1,128]{1,0:T(2,128)(2,1)} %get-tuple-element.61), channel_id=1, source_target_pairs={{0,1},{2,3},{4,5},{6,7},{8,9},{10,11},{12,13},{14,15},{16,17},{18,... | collective-permute-start | bytes 776 | tf_op jit(solution)/shard_map/ppermute | solution.py:14
  20.3 17.6 %collective-permute-start = (bf16[1,128,768]{2,1,0:T(8,128)(2,1)}, bf16[1,128,768]{2,1,0:T(8,128)(2,1)}, u32[]{:S(2)}, u32[]{:S(2)}) collective-permute-start(bf16[1,128,768]{2,1,0:T(8,128)(2,1)} %get-tuple-element.57), channel_id=1, source_target_pairs={{0,1},{2,3},{4,5},{6,7},{8,9},{10,11},{12,13},{14,15},{16,17},{18,... | collective-permute-start | bytes 589832 | tf_op jit(solution)/shard_map/ppermute | solution.py:14
  24.0 21.6 %copy-start.36 = (f32[768]{0:T(1024)}, f32[768]{0:T(1024)S(1)}, u32[]{:S(2)}) copy-start(f32[768]{0:T(1024)S(1)} %get-tuple-element.82) | copy-start | bytes 9220
  54.1 2.1 collective-permute-start.3
  60.5 2.8 copy-start.32
  65.4 12.2 %collective-permute-start.6 = (bf16[1,128,768]{2,1,0:T(8,128)(2,1)}, bf16[1,128,768]{2,1,0:T(8,128)(2,1)}, u32[]{:S(2)}, u32[]{:S(2)}) collective-permute-start(bf16[1,128,768]{2,1,0:T(8,128)(2,1)} %get-tuple-element.52), channel_id=1, source_target_pairs={{0,1},{2,3},{4,5},{6,7},{8,9},{10,11},{12,13},{14,15},{16,17},{18,... | collective-permute-start | bytes 589832 | tf_op jit(solution)/shard_map/ppermute | solution.py:14
  68.3 7.3 collective-permute-start.4
  71.3 13.3 %collective-permute-start.5 = (bf16[1,128,768]{2,1,0:T(8,128)(2,1)}, bf16[1,128,768]{2,1,0:T(8,128)(2,1)}, u32[]{:S(2)}, u32[]{:S(2)}) collective-permute-start(bf16[1,128,768]{2,1,0:T(8,128)(2,1)} %get-tuple-element.54), channel_id=1, source_target_pairs={{0,1},{2,3},{4,5},{6,7},{8,9},{10,11},{12,13},{14,15},{16,17},{18,... | collective-permute-start | bytes 589832 | tf_op jit(solution)/shard_map/ppermute | solution.py:14
  81.3 3.3 copy-start.23
  90.9 11.5 %copy-start.7 = (f32[128,768]{1,0:T(8,128)}, f32[128,768]{1,0:T(8,128)S(1)}, u32[]{:S(2)}) copy-start(f32[128,768]{1,0:T(8,128)S(1)} %get-tuple-element.73) | copy-start | bytes 1179652
  90.9 11.5 %copy-start.41 = (f32[128]{0:T(128)}, f32[128]{0:T(128)S(1)}, u32[]{:S(2)}) copy-start(f32[128]{0:T(128)S(1)} %broadcast_multiply_fusion.1) | copy-start | bytes 1540
  91.1 11.3 %copy-start.48 = (f32[128]{0:T(128)}, f32[128]{0:T(128)S(1)}, u32[]{:S(2)}) copy-start(f32[128]{0:T(128)S(1)} %fusion.112) | copy-start | bytes 1540
  91.1 3.4 copy-start.18
  91.1 8.9 slice-start
  94.5 5.5 copy-start.11
  94.5 5.5 slice-start.1
  108.9 226.1 %reduce-scatter.8.cloned.1.call-start = ((), (), s32[]{:S(2)}) async-start(), calls=%async_computation.6 | async-start | bytes 7299072 | tf_op jit(solution)/shard_map/reduce_scatter | solution.py:344
  117.0 3.4 copy-start.17
  117.1 3.9 collective-permute-start.7
  119.0 4.3 copy-start.5
  119.0 4.3 copy-start.35
  119.0 4.2 copy-start.46
  119.0 4.2 copy-start.51
  119.1 3.5 collective-permute-start.8
  134.7 341.7 %reduce-scatter.12.cloned.1.call-start = ((), (), s32[]{:S(2)}) async-start(), calls=%async_computation.10 | async-start | bytes 9732096 | tf_op jit(solution)/shard_map/reduce_scatter | solution.py:346
  151.1 466.4 %reduce-scatter.14.cloned.1.call-start = ((), (), s32[]{:S(2)}) async-start(), calls=%async_computation.12 | async-start | bytes 9732096 | tf_op jit(solution)/shard_map/reduce_scatter | solution.py:347
  167.3 453.7 %all-reduce.9.cloned.1.call-start = ((), (), s32[]{:S(2)}) async-start(), calls=%async_computation.15 | async-start | bytes 884736 | tf_op jit(solution)/shard_map/psum | solution.py:324
  169.3 3.4 copy-start.57
  169.3 3.4 copy-start.6
  169.3 3.7 copy-start.16
  174.7 537.6 %all-gather.7.cloned.1.call-start = ((), (), s32[]{:S(2)}) async-start(), calls=%async_computation.9 | async-start | bytes 1216512 | tf_op jit(solution)/shard_map/all_gather | solution.py:353
  211.7 414.2 %copy-start.44 = (f32[768]{0:T(1024)S(1)}, f32[768]{0:T(1024)}, u32[]{:S(2)}) copy-start(f32[768]{0:T(1024)} %get-tuple-element.19) | copy-start | bytes 9220
  211.7 414.8 %copy-start.43 = (f32[768]{0:T(1024)S(1)}, f32[768]{0:T(1024)}, u32[]{:S(2)}) copy-start(f32[768]{0:T(1024)} %get-tuple-element.23) | copy-start | bytes 9220
  211.7 529.4 %all-gather.5.cloned.1.call-start = ((), (), s32[]{:S(2)}) async-start(), calls=%async_computation.7 | async-start | bytes 3649536 | tf_op jit(solution)/shard_map/all_gather | solution.py:350
  336.6 473.1 %all-gather.9.cloned.1.call-start = ((), (), s32[]{:S(2)}) async-start(), calls=%async_computation.11 | async-start | bytes 4866048 | tf_op jit(solution)/shard_map/all_gather | solution.py:356
  478.0 399.5 %all-gather.11.cloned.1.call-start = ((), (), s32[]{:S(2)}) async-start(), calls=%async_computation.13 | async-start | bytes 4866048 | tf_op jit(solution)/shard_map/all_gather | solution.py:359
  621.0 264.4 %all-reduce.7.cloned.1.call-start = ((), (), s32[]{:S(2)}) async-start(), calls=%async_computation.14 | async-start | bytes 1671168 | tf_op jit(solution)/shard_map/psum | solution.py:323
  621.6 279.4 %reduce-scatter.6.cloned.1.call-start = ((), (), s32[]{:S(2)}) async-start(), calls=%async_computation.5 | async-start | bytes 3342336 | tf_op jit(solution)/shard_map/reduce_scatter | solution.py:312
  (34 other events, 43.2 us)
Sparse Core Ops, SparseCore 0:
  109.0 101.0 reduce-scatter.9
  216.8 118.1 reduce-scatter.7
  341.4 134.8 reduce-scatter.11
  483.1 134.3 reduce-scatter.13
  620.8 55.5 all-gather.6
  679.8 61.2 all-gather.4
  744.5 65.0 all-gather.8
  812.5 64.8 all-gather.10
Sparse Core Ops, SparseCore 1:
  174.8 20.1 all-reduce.8
  628.7 115.1 all-reduce.6
  749.3 151.7 reduce-scatter.5
